TPU v7x, 32 devices: a whole 2x2x4 slice. The times are simulated.
32 devices in a mesh: uly: 8 (over z, y), blk: 4 (over x, core).
Axes of the slice: x: 2, y: 2, z: 4, core: 2. Of those that a mesh axis runs over, the one named last changes fastest.
Arguments:
- queries: bfloat16 [2048, 2048], P(('blk', 'uly')), may hold values from -20 to 20
- keys: bfloat16 [2048, 2048], P(('blk', 'uly')), may hold values from -20 to 20
- values: bfloat16 [2048, 2048], P(('blk', 'uly')), may hold values from -6 to 6
- block_list: int32 [32, 16, 16], P('uly', 'blk'), may hold values from -1 to 15, as said below
Outputs:
- attended: bfloat16 [2048, 2048], P(('blk', 'uly'))
Inputs may be any that keep to these rules, and one draw needn't show every extreme that they name: block_list[h, b, 0] = b; every other entry is -1 (an empty slot) or a block below b, and the blocks named in one list are distinct.
All inputs are finite; a program needn't handle non-finite values.
Results may differ from a plain program's by a relative error of at most 0.0045.
Values may be sent and summed in bfloat16 or wider, within the bound.
No kernel may reach another device: no remote copies, remote signals or barrier semaphores. Data moves between devices by JAX's collectives and lax.ppermute only.
A program may use at most 64 MiB of HBM per device.

v0:
```python
import jax
import jax.numpy as jnp
from jax import lax
from jax.sharding import PartitionSpec as P

BLOCK = 128
QGROUP = 2


def head_major(token_rows, heads_local, head_dim):
    return token_rows.reshape(token_rows.shape[0] // BLOCK, BLOCK, heads_local, head_dim).transpose(
        2, 0, 1, 3
    )


def select_blocks(source, chosen):
    return jnp.take(source, chosen, axis=0)


def attend_block(operand):
    query_group, key_slots, value_slots, chosen, query_block = operand
    scale = query_group.shape[-1] ** (-0.5)
    scores = (
        jnp.einsum("abd,asjd->absj", query_group, key_slots, preferred_element_type=jnp.float32)
        * scale
    )
    positions = jnp.arange(BLOCK, dtype=jnp.int32)
    query_pos = query_block[:, None] * BLOCK + positions[None, :]
    key_pos = jnp.maximum(chosen, 0)[:, :, None] * BLOCK + positions[None, None, :]
    allowed = (chosen[:, None, :, None] >= 0) & (
        key_pos[:, None, :, :] <= query_pos[:, :, None, None]
    )
    scores = jnp.where(allowed, scores, -1e30)
    row_max = jnp.max(scores, axis=(2, 3), keepdims=True)
    weights = jnp.where(allowed, jnp.exp(scores - row_max), 0.0)
    denominator = jnp.sum(weights, axis=(2, 3))
    rounded = weights.astype(jnp.bfloat16)
    summed = jnp.einsum("absj,asjd->abd", rounded, value_slots, preferred_element_type=jnp.float32)
    return (summed / denominator[:, :, None]).astype(jnp.bfloat16)


def local(queries, keys, values, block_list):
    heads_local = block_list.shape[0]
    blocks_dev = block_list.shape[1]
    slot_count = block_list.shape[2]
    head_dim = queries.shape[1] // (heads_local * lax.axis_size("uly"))
    first_block = lax.axis_index("blk") * blocks_dev
    query_rows, key_rows, value_rows = (
        lax.all_to_all(queries, "uly", split_axis=1, concat_axis=0, tiled=True),
        lax.all_to_all(keys, "uly", split_axis=1, concat_axis=0, tiled=True),
        lax.all_to_all(values, "uly", split_axis=1, concat_axis=0, tiled=True),
    )
    keys_all = lax.all_gather(key_rows, "blk", axis=0, tiled=True)
    values_all = lax.all_gather(value_rows, "blk", axis=0, tiled=True)
    chosen = jnp.maximum(block_list, 0)
    key_slots = jax.vmap(select_blocks)(head_major(keys_all, heads_local, head_dim), chosen)
    value_slots = jax.vmap(select_blocks)(head_major(values_all, heads_local, head_dim), chosen)
    key_slots, value_slots = (key_slots, value_slots)
    groups = heads_local * blocks_dev // QGROUP
    query_heads = head_major(query_rows, heads_local, head_dim).reshape(
        groups, QGROUP, BLOCK, head_dim
    )
    key_groups = key_slots.reshape(groups, QGROUP, slot_count, BLOCK, head_dim)
    value_groups = value_slots.reshape(groups, QGROUP, slot_count, BLOCK, head_dim)
    list_groups = block_list.reshape(groups, QGROUP, slot_count)
    block_numbers = first_block + jnp.arange(blocks_dev, dtype=jnp.int32)
    block_groups = jnp.broadcast_to(block_numbers[None, :], (heads_local, blocks_dev)).reshape(
        groups, QGROUP
    )
    result = lax.map(
        attend_block, (query_heads, key_groups, value_groups, list_groups, block_groups)
    )
    result = result.reshape(heads_local, blocks_dev * BLOCK, head_dim).transpose(1, 0, 2)
    result = result.reshape(blocks_dev * BLOCK, heads_local * head_dim)
    return lax.all_to_all(result, "uly", split_axis=0, concat_axis=1, tiled=True)


def solution(mesh):
    placed = (
        P(("blk", "uly"), None),
        P(("blk", "uly"), None),
        P(("blk", "uly"), None),
        P("uly", "blk", None),
    )
    return jax.shard_map(
        local, mesh=mesh, in_specs=placed, out_specs=P(("blk", "uly"), None), check_vma=False
    )
```

profile of v0, /device:TPU:0, one launch (start us, length us, event | category | flops | bytes accessed | tf_op | source)
XLA Modules:
  0.0 148.7 jit_solution(14057702400680355051)
XLA Ops:
  6.5 1.0 copy.82
  7.6 16.1 %all_to_all.73 = bf16[64,8,256]{2,0,1:T(8,128)(2,1)} all-to-all(bf16[64,8,256]{2,0,1:T(8,128)(2,1)S(1)} %bitcast.102), channel_id=1, replica_groups=mesh['uly'=8,'blk'=4] {'uly'}, dimensions={1} | all-to-all | bytes 524288 | tf_op jit(solution)/shard_map/all_to_all | solution.py:50
  23.8 1.0 copy.81
  24.7 12.1 %all_to_all.74 = bf16[64,8,256]{2,0,1:T(8,128)(2,1)} all-to-all(bf16[64,8,256]{2,0,1:T(8,128)(2,1)S(1)} %bitcast.103), channel_id=1, replica_groups=mesh['uly'=8,'blk'=4] {'uly'}, dimensions={1} | all-to-all | bytes 524288 | tf_op jit(solution)/shard_map/all_to_all | solution.py:51
  36.8 0.7 copy.83
  37.5 3.6 %all-to-all-start = ((bf16[64,8,256]{2,0,1:T(8,128)(2,1)}), bf16[64,8,256]{2,0,1:T(8,128)(2,1)S(1)}, u32[]{:S(2)}, u32[]{:S(2)}) async-start(bf16[64,8,256]{2,0,1:T(8,128)(2,1)} %bitcast.73), calls=%async_computation | async-start | bytes 524288 | tf_op jit(solution)/shard_map/all_to_all | solution.py:49
  41.1 0.1 reshape.139
  41.2 0.1 copy.72
  41.3 8.3 %all-to-all-done = bf16[64,8,256]{2,0,1:T(8,128)(2,1)S(1)} async-done(((bf16[64,8,256]{2,0,1:T(8,128)(2,1)}), bf16[64,8,256]{2,0,1:T(8,128)(2,1)S(1)}, u32[]{:S(2)}, u32[]{:S(2)}) %all-to-all-start) | async-done | bytes 262176 | tf_op jit(solution)/shard_map/all_to_all | solution.py:49
  49.7 0.2 reshape.150
  49.9 0.3 copy.46
  50.3 3.3 %reshape.151 = bf16[16,128,4,64]{3,2,1,0:T(4,128)(2,1)S(1)} reshape(bf16[2048,256]{1,0:T(8,128)(2,1)} %all-gather.3.cloned.1.call-done) | data formatting | bytes 2097152 | tf_op jit(solution)/shard_map/reshape | solution.py:11
  53.6 1.4 copy.49
  55.0 2.8 %all-gather.5.cloned.1.call-done = bf16[2048,256]{1,0:T(8,128)(2,1)} async-done(((bf16[512,256]{1,0:T(8,128)(2,1)}), bf16[2048,256]{1,0:T(8,128)(2,1)}) %all-gather.5.cloned.1.call-update) | async-done | bytes 1048592 | tf_op jit(solution)/shard_map/all_gather | solution.py:54
  57.9 4.4 %reshape.152 = bf16[16,128,4,64]{3,2,1,0:T(4,128)(2,1)} reshape(bf16[2048,256]{1,0:T(8,128)(2,1)} %all-gather.5.cloned.1.call-done) | data formatting | bytes 2097152 | tf_op jit(solution)/shard_map/reshape | solution.py:11
  62.3 3.0 %copy.52 = bf16[16,128,4,64]{1,3,0,2:T(8,128)(2,1)S(1)} copy(bf16[16,128,4,64]{3,2,1,0:T(4,128)(2,1)} %reshape.152) | data formatting | bytes 2097152 | tf_op jit(solution)/shard_map/reshape | solution.py:11
  65.3 3.3 %gather_fusion = bf16[256,128,64]{1,2,0:T(8,128)(2,1)} fusion(bf16[4,16,128,64]{2,3,1,0:T(8,128)(2,1)S(1)} %bitcast.90, s32[256]{0:T(256)S(1)} %reshape.139), kind=kCustom, calls=%fused_computation.clone | custom fusion | bytes 8390656 | tf_op jit(solution)/shard_map/vmap(jit(_take))/gather | solution.py:17
  68.6 3.3 %gather_fusion.1 = bf16[256,128,64]{1,2,0:T(8,128)(2,1)} fusion(bf16[4,16,128,64]{2,3,1,0:T(8,128)(2,1)S(1)} %bitcast.91, s32[256]{0:T(256)S(1)} %reshape.139), kind=kCustom, calls=%fused_computation.1.clone | custom fusion | bytes 8390656 | tf_op jit(solution)/shard_map/vmap(jit(_take))/gather | solution.py:17
  72.0 5.9 %broadcast_select_fusion = (bf16[4,4,16,128,64]{3,4,2,1,0:T(8,128)(2,1)}, bf16[4,4,16,128,64]{3,4,2,1,0:T(8,128)(2,1)}) fusion(bf16[4,4,16,128,64]{3,4,2,1,0:T(8,128)(2,1)} %bitcast.93, pred[4,4,16]{2,1,0:T(4,128)(4,1)S(1)} %maximum_compare_fusion, bf16[4,4,16,128,64]{3,4,2,1,0:T(8,128)(2,1)} %bitcast.92), kind=kLoop, calls=%fused_computation.33 | loop fusion | flops 4194304 | bytes 16777472 | tf_op jit(solution)/shard_map/vmap(jit(_take))/select_n | solution.py:17
  77.9 47.7 %while.10 = (s32[]{:T(128)}, bf16[8,2,128,64]{2,1,0,3:T(2,128)(2,1)S(1)}, s32[8,2,16]{2,1,0:T(2,128)S(1)}, s32[8,2]{1,0:T(8,128)S(1)}, bf16[8,2,128,64]{2,3,1,0:...) while((s32[]{:T(128)}, ...), condition=%wide.region_3.5_spmd, body=%wide.region_0.4_spmd.sunk | while | flops 142118752 | bytes 7548637 | solution.py:70
  78.0 0.1 iota_add_fusion.5
  78.1 0.1 iota_add_fusion.4
  78.1 2.9 %fusion.31 = (f32[2,128]{1,0:T(2,128)S(1)}, f32[2,128,16,128]{1,3,2,0:T(8,128)S(1)}) fusion(bf16[8,2,16,128,64]{3,4,2,1,0:T(8,128)(2,1)} %get-tuple-element.165, s32[]{:T(128)} %get-tuple-element.152, bf16[8,2,128,64]{2,3,1,0:T(8,128)(2,1)S(1)} %get-tuple-element.164, s32[2,128]{1,0:T(2,128)S(1)} %iota_add_fusion.4, ...), kind=kOutput, calls=%fused_computation.41.clone.1 | convolution fusion | flops 69730048 | bytes 2674176 | tf_op jit(solution)/shard_map/while/body/eval_jaxpr/abd,asjd->absj/dot_general | solution.py:24
  81.0 0.8 fusion.32
  81.8 2.1 %fusion.33 = bf16[1,2,128,64]{2,3,1,0:T(8,128)(2,1)S(1)} fusion(f32[2,128,16,128]{1,3,2,0:T(8,128)S(1)} %get-tuple-element.142, f32[2,128]{1,0:T(2,128)S(1)} %get-tuple-element.143, s32[2,128]{1,0:T(2,128)S(1)} %iota_add_fusion.4, s32[2,16,128]{2,1,0:T(8,128)S(1)} %iota_add_fusion.5, pred[2,16]{1,0:T(4,128)(4,1)S(1)} %compare_bitcast_fusion.2, ...), kind=kOutput, calls=%fused_computation.10.clone.1 | convolution fusion | flops 69763072 | bytes 2674208 | tf_op jit(solution)/shard_map/while/body/eval_jaxpr/absj,asjd->abd/dot_general | solution.py:38
  83.9 0.1 iota_add_fusion.5
  84.0 0.1 iota_add_fusion.4
  84.1 2.9 %fusion.31 = (f32[2,128]{1,0:T(2,128)S(1)}, f32[2,128,16,128]{1,3,2,0:T(8,128)S(1)}) fusion(bf16[8,2,16,128,64]{3,4,2,1,0:T(8,128)(2,1)} %get-tuple-element.165, s32[]{:T(128)} %get-tuple-element.152, bf16[8,2,128,64]{2,3,1,0:T(8,128)(2,1)S(1)} %get-tuple-element.164, s32[2,128]{1,0:T(2,128)S(1)} %iota_add_fusion.4, ...), kind=kOutput, calls=%fused_computation.41.clone.1 | convolution fusion | flops 69730048 | bytes 2674176 | tf_op jit(solution)/shard_map/while/body/eval_jaxpr/abd,asjd->absj/dot_general | solution.py:24
  87.0 0.8 fusion.32
  87.7 2.1 %fusion.33 = bf16[1,2,128,64]{2,3,1,0:T(8,128)(2,1)S(1)} fusion(f32[2,128,16,128]{1,3,2,0:T(8,128)S(1)} %get-tuple-element.142, f32[2,128]{1,0:T(2,128)S(1)} %get-tuple-element.143, s32[2,128]{1,0:T(2,128)S(1)} %iota_add_fusion.4, s32[2,16,128]{2,1,0:T(8,128)S(1)} %iota_add_fusion.5, pred[2,16]{1,0:T(4,128)(4,1)S(1)} %compare_bitcast_fusion.2, ...), kind=kOutput, calls=%fused_computation.10.clone.1 | convolution fusion | flops 69763072 | bytes 2674208 | tf_op jit(solution)/shard_map/while/body/eval_jaxpr/absj,asjd->abd/dot_general | solution.py:38
  89.9 0.1 iota_add_fusion.5
  90.0 0.1 iota_add_fusion.4
  90.1 2.9 %fusion.31 = (f32[2,128]{1,0:T(2,128)S(1)}, f32[2,128,16,128]{1,3,2,0:T(8,128)S(1)}) fusion(bf16[8,2,16,128,64]{3,4,2,1,0:T(8,128)(2,1)} %get-tuple-element.165, s32[]{:T(128)} %get-tuple-element.152, bf16[8,2,128,64]{2,3,1,0:T(8,128)(2,1)S(1)} %get-tuple-element.164, s32[2,128]{1,0:T(2,128)S(1)} %iota_add_fusion.4, ...), kind=kOutput, calls=%fused_computation.41.clone.1 | convolution fusion | flops 69730048 | bytes 2674176 | tf_op jit(solution)/shard_map/while/body/eval_jaxpr/abd,asjd->absj/dot_general | solution.py:24
  92.9 0.8 fusion.32
  93.7 2.1 %fusion.33 = bf16[1,2,128,64]{2,3,1,0:T(8,128)(2,1)S(1)} fusion(f32[2,128,16,128]{1,3,2,0:T(8,128)S(1)} %get-tuple-element.142, f32[2,128]{1,0:T(2,128)S(1)} %get-tuple-element.143, s32[2,128]{1,0:T(2,128)S(1)} %iota_add_fusion.4, s32[2,16,128]{2,1,0:T(8,128)S(1)} %iota_add_fusion.5, pred[2,16]{1,0:T(4,128)(4,1)S(1)} %compare_bitcast_fusion.2, ...), kind=kOutput, calls=%fused_computation.10.clone.1 | convolution fusion | flops 69763072 | bytes 2674208 | tf_op jit(solution)/shard_map/while/body/eval_jaxpr/absj,asjd->abd/dot_general | solution.py:38
  95.9 0.1 iota_add_fusion.5
  96.0 0.1 iota_add_fusion.4
  96.0 2.9 %fusion.31 = (f32[2,128]{1,0:T(2,128)S(1)}, f32[2,128,16,128]{1,3,2,0:T(8,128)S(1)}) fusion(bf16[8,2,16,128,64]{3,4,2,1,0:T(8,128)(2,1)} %get-tuple-element.165, s32[]{:T(128)} %get-tuple-element.152, bf16[8,2,128,64]{2,3,1,0:T(8,128)(2,1)S(1)} %get-tuple-element.164, s32[2,128]{1,0:T(2,128)S(1)} %iota_add_fusion.4, ...), kind=kOutput, calls=%fused_computation.41.clone.1 | convolution fusion | flops 69730048 | bytes 2674176 | tf_op jit(solution)/shard_map/while/body/eval_jaxpr/abd,asjd->absj/dot_general | solution.py:24
  98.9 0.8 fusion.32
  99.7 2.1 %fusion.33 = bf16[1,2,128,64]{2,3,1,0:T(8,128)(2,1)S(1)} fusion(f32[2,128,16,128]{1,3,2,0:T(8,128)S(1)} %get-tuple-element.142, f32[2,128]{1,0:T(2,128)S(1)} %get-tuple-element.143, s32[2,128]{1,0:T(2,128)S(1)} %iota_add_fusion.4, s32[2,16,128]{2,1,0:T(8,128)S(1)} %iota_add_fusion.5, pred[2,16]{1,0:T(4,128)(4,1)S(1)} %compare_bitcast_fusion.2, ...), kind=kOutput, calls=%fused_computation.10.clone.1 | convolution fusion | flops 69763072 | bytes 2674208 | tf_op jit(solution)/shard_map/while/body/eval_jaxpr/absj,asjd->abd/dot_general | solution.py:38
  101.8 0.1 iota_add_fusion.5
  102.0 2.9 %fusion.31 = (f32[2,128]{1,0:T(2,128)S(1)}, f32[2,128,16,128]{1,3,2,0:T(8,128)S(1)}) fusion(bf16[8,2,16,128,64]{3,4,2,1,0:T(8,128)(2,1)} %get-tuple-element.165, s32[]{:T(128)} %get-tuple-element.152, bf16[8,2,128,64]{2,3,1,0:T(8,128)(2,1)S(1)} %get-tuple-element.164, s32[2,128]{1,0:T(2,128)S(1)} %iota_add_fusion.4, ...), kind=kOutput, calls=%fused_computation.41.clone.1 | convolution fusion | flops 69730048 | bytes 2674176 | tf_op jit(solution)/shard_map/while/body/eval_jaxpr/abd,asjd->absj/dot_general | solution.py:24
  104.9 0.8 fusion.32
  105.6 2.1 %fusion.33 = bf16[1,2,128,64]{2,3,1,0:T(8,128)(2,1)S(1)} fusion(f32[2,128,16,128]{1,3,2,0:T(8,128)S(1)} %get-tuple-element.142, f32[2,128]{1,0:T(2,128)S(1)} %get-tuple-element.143, s32[2,128]{1,0:T(2,128)S(1)} %iota_add_fusion.4, s32[2,16,128]{2,1,0:T(8,128)S(1)} %iota_add_fusion.5, pred[2,16]{1,0:T(4,128)(4,1)S(1)} %compare_bitcast_fusion.2, ...), kind=kOutput, calls=%fused_computation.10.clone.1 | convolution fusion | flops 69763072 | bytes 2674208 | tf_op jit(solution)/shard_map/while/body/eval_jaxpr/absj,asjd->abd/dot_general | solution.py:38
  107.8 0.1 iota_add_fusion.5
  107.9 0.1 iota_add_fusion.4
  108.0 2.9 %fusion.31 = (f32[2,128]{1,0:T(2,128)S(1)}, f32[2,128,16,128]{1,3,2,0:T(8,128)S(1)}) fusion(bf16[8,2,16,128,64]{3,4,2,1,0:T(8,128)(2,1)} %get-tuple-element.165, s32[]{:T(128)} %get-tuple-element.152, bf16[8,2,128,64]{2,3,1,0:T(8,128)(2,1)S(1)} %get-tuple-element.164, s32[2,128]{1,0:T(2,128)S(1)} %iota_add_fusion.4, ...), kind=kOutput, calls=%fused_computation.41.clone.1 | convolution fusion | flops 69730048 | bytes 2674176 | tf_op jit(solution)/shard_map/while/body/eval_jaxpr/abd,asjd->absj/dot_general | solution.py:24
  110.8 0.8 fusion.32
  111.6 2.1 %fusion.33 = bf16[1,2,128,64]{2,3,1,0:T(8,128)(2,1)S(1)} fusion(f32[2,128,16,128]{1,3,2,0:T(8,128)S(1)} %get-tuple-element.142, f32[2,128]{1,0:T(2,128)S(1)} %get-tuple-element.143, s32[2,128]{1,0:T(2,128)S(1)} %iota_add_fusion.4, s32[2,16,128]{2,1,0:T(8,128)S(1)} %iota_add_fusion.5, pred[2,16]{1,0:T(4,128)(4,1)S(1)} %compare_bitcast_fusion.2, ...), kind=kOutput, calls=%fused_computation.10.clone.1 | convolution fusion | flops 69763072 | bytes 2674208 | tf_op jit(solution)/shard_map/while/body/eval_jaxpr/absj,asjd->abd/dot_general | solution.py:38
  113.8 0.1 iota_add_fusion.5
  113.9 0.1 iota_add_fusion.4
  113.9 2.9 %fusion.31 = (f32[2,128]{1,0:T(2,128)S(1)}, f32[2,128,16,128]{1,3,2,0:T(8,128)S(1)}) fusion(bf16[8,2,16,128,64]{3,4,2,1,0:T(8,128)(2,1)} %get-tuple-element.165, s32[]{:T(128)} %get-tuple-element.152, bf16[8,2,128,64]{2,3,1,0:T(8,128)(2,1)S(1)} %get-tuple-element.164, s32[2,128]{1,0:T(2,128)S(1)} %iota_add_fusion.4, ...), kind=kOutput, calls=%fused_computation.41.clone.1 | convolution fusion | flops 69730048 | bytes 2674176 | tf_op jit(solution)/shard_map/while/body/eval_jaxpr/abd,asjd->absj/dot_general | solution.py:24
  116.8 0.8 fusion.32
  117.6 2.1 %fusion.33 = bf16[1,2,128,64]{2,3,1,0:T(8,128)(2,1)S(1)} fusion(f32[2,128,16,128]{1,3,2,0:T(8,128)S(1)} %get-tuple-element.142, f32[2,128]{1,0:T(2,128)S(1)} %get-tuple-element.143, s32[2,128]{1,0:T(2,128)S(1)} %iota_add_fusion.4, s32[2,16,128]{2,1,0:T(8,128)S(1)} %iota_add_fusion.5, pred[2,16]{1,0:T(4,128)(4,1)S(1)} %compare_bitcast_fusion.2, ...), kind=kOutput, calls=%fused_computation.10.clone.1 | convolution fusion | flops 69763072 | bytes 2674208 | tf_op jit(solution)/shard_map/while/body/eval_jaxpr/absj,asjd->abd/dot_general | solution.py:38
  119.7 0.1 iota_add_fusion.5
  119.8 0.1 iota_add_fusion.4
  119.9 2.9 %fusion.31 = (f32[2,128]{1,0:T(2,128)S(1)}, f32[2,128,16,128]{1,3,2,0:T(8,128)S(1)}) fusion(bf16[8,2,16,128,64]{3,4,2,1,0:T(8,128)(2,1)} %get-tuple-element.165, s32[]{:T(128)} %get-tuple-element.152, bf16[8,2,128,64]{2,3,1,0:T(8,128)(2,1)S(1)} %get-tuple-element.164, s32[2,128]{1,0:T(2,128)S(1)} %iota_add_fusion.4, ...), kind=kOutput, calls=%fused_computation.41.clone.1 | convolution fusion | flops 69730048 | bytes 2674176 | tf_op jit(solution)/shard_map/while/body/eval_jaxpr/abd,asjd->absj/dot_general | solution.py:24
  122.8 0.8 fusion.32
  123.5 2.1 %fusion.33 = bf16[1,2,128,64]{2,3,1,0:T(8,128)(2,1)S(1)} fusion(f32[2,128,16,128]{1,3,2,0:T(8,128)S(1)} %get-tuple-element.142, f32[2,128]{1,0:T(2,128)S(1)} %get-tuple-element.143, s32[2,128]{1,0:T(2,128)S(1)} %iota_add_fusion.4, s32[2,16,128]{2,1,0:T(8,128)S(1)} %iota_add_fusion.5, pred[2,16]{1,0:T(4,128)(4,1)S(1)} %compare_bitcast_fusion.2, ...), kind=kOutput, calls=%fused_computation.10.clone.1 | convolution fusion | flops 69763072 | bytes 2674208 | tf_op jit(solution)/shard_map/while/body/eval_jaxpr/absj,asjd->abd/dot_general | solution.py:38
  125.7 0.1 reshape.115
  125.8 0.4 copy.68
  126.2 0.3 reshape.153
  126.5 14.6 %all_to_all.75 = bf16[8,64,256]{2,1,0:T(8,128)(2,1)S(1)} all-to-all(bf16[8,64,256]{2,1,0:T(8,128)(2,1)S(1)} %reshape.153), channel_id=1, replica_groups=mesh['uly'=8,'blk'=4] {'uly'}, dimensions={0} | all-to-all | bytes 524288 | tf_op jit(solution)/shard_map/all_to_all | solution.py:75
  141.1 0.7 copy.76
  (49 shorter events, 0.9 us)
Async XLA Ops:
  6.5 30.3 %copy-start = (bf16[64,2048]{1,0:T(8,128)(2,1)S(1)}, bf16[64,2048]{1,0:T(8,128)(2,1)}, u32[]{:S(2)}) copy-start(bf16[64,2048]{1,0:T(8,128)(2,1)} %param.8) | copy-start | bytes 786436
  6.5 34.6 %copy-start.2 = (s32[4,4,16]{2,1,0:T(4,128)S(1)}, s32[4,4,16]{2,1,0:T(4,128)}, u32[]{:S(2)}) copy-start(s32[4,4,16]{2,1,0:T(4,128)} %param.11) | copy-start | bytes 3076
  6.5 43.7 %all-gather.3.cloned.1.call-start = ((), (), s32[]{:S(2)}) async-start(), calls=%async_computation.4 | async-start | bytes 1310720 | tf_op jit(solution)/shard_map/all_gather | solution.py:53
  23.7 34.1 %all-gather.5.cloned.1.call-start = ((), (), s32[]{:S(2)}) async-start(), calls=%async_computation.5 | async-start | bytes 1310720 | tf_op jit(solution)/shard_map/all_gather | solution.py:54
  37.5 12.1 %all-to-all-start = ((bf16[64,8,256]{2,0,1:T(8,128)(2,1)}), bf16[64,8,256]{2,0,1:T(8,128)(2,1)S(1)}, u32[]{:S(2)}, u32[]{:S(2)}) async-start(bf16[64,8,256]{2,0,1:T(8,128)(2,1)} %bitcast.73), calls=%async_computation | async-start | bytes 524288 | tf_op jit(solution)/shard_map/all_to_all | solution.py:49
  72.0 6.0 %copy-start.1 = (bf16[8,2,128,64]{2,1,0,3:T(2,128)(2,1)S(1)}, bf16[8,2,128,64]{2,1,0,3:T(2,128)(2,1)}, u32[]{:S(2)}) copy-start(bf16[8,2,128,64]{2,1,0,3:T(2,128)(2,1)} %custom-call.6) | copy-start | bytes 786436
Sparse Core Ops, SparseCore 0:
  23.8 15.6 all-gather.2
  41.1 16.6 all-gather.4
where the time goes:
time: 150 us; the launch traced here: 149 us
  blocking collectives  42.8 us (29%)
  matrix products  39.3 us (26%)
  local copies, waits for them, and re-layouts  24.3 us (16%)
  other arithmetic  13.5 us (9%)
  between operations  13.5 us (9%)
  waiting for transfers between devices  11.2 us (7%)
  starting transfers between devices  3.63 us (2%)
    dot_general x8, matrix products, attend_block(): jnp.einsum('abd,asjd->absj', query_group, key_slots, preferred_element_ty...  22.8 us
    dot_general x8, matrix products, attend_block(): jnp.einsum('absj,asjd->abd', rounded, value_slots, preferred_element_type...  16.4 us
    all_to_all x1, blocking collectives, local(): lax.all_to_all(keys, 'uly', split_axis=1, concat_axis=0, tiled=True)  16.1 us
    all_to_all x1, blocking collectives, local(): lax.all_to_all(result, 'uly', split_axis=0, concat_axis=1, tiled=True)  14.6 us
    reshape x5, local copies, waits for them, and re-layouts, head_major(): token_rows.reshape(token_rows.shape[0] // BLOCK, BLOCK, heads_local, head...  12.4 us
    all_to_all x1, blocking collectives, local(): lax.all_to_all(values, 'uly', split_axis=1, concat_axis=0, tiled=True)  12.1 us
    all_to_all x1, waiting for transfers between devices, local(): lax.all_to_all(queries, 'uly', split_axis=1, concat_axis=0, tiled=True)  8.31 us
    gather x3, local copies, waits for them, and re-layouts, select_blocks(): return jnp.take(source, chosen, axis=0)  6.75 us
  transfers between devices with their start and end apart: 3, of which 2 were waited for; matrix products, arithmetic and copies ran while one was open for 5% of the time, Pallas kernels for 0%

commit v1 on v0

--- a/solution.py
+++ b/solution.py
@@ -1,3 +1,4 @@
+import functools
 import jax
 import jax.numpy as jnp
 from jax import lax
@@ -5,6 +6,28 @@
 
 BLOCK = 128
 QGROUP = 2
+
+
+def start_the_groups(row_data, along_axis):
+    piece_next, block_out = (lax.psum(1, axis_name=along_axis), lax.axis_index(along_axis))
+    earlier = row_data.shape[1] // piece_next
+    y1 = list(row_data.shape)
+    y1[1] = earlier
+    spare = y1[0]
+    y1[0] = spare * piece_next
+    a_now = jnp.zeros(y1, row_data.dtype)
+    for c in [*range(piece_next)]:
+        block_now = lax.dynamic_slice_in_dim(row_data, (block_out ^ c) * earlier, earlier, axis=1)
+        if c:
+            tray = []
+            for w in [*range(piece_next)]:
+                tray.append((w, w ^ c))
+            block_now = lax.ppermute(block_now, axis_name=along_axis, perm=tray)
+        a_now = lax.dynamic_update_slice_in_dim(a_now, block_now, (block_out ^ c) * spare, axis=0)
+    return a_now
+
+
+recast_the_chains = functools.partial(start_the_groups, along_axis="uly")
 
 
 def head_major(token_rows, heads_local, head_dim):
@@ -46,7 +69,7 @@
     head_dim = queries.shape[1] // (heads_local * lax.axis_size("uly"))
     first_block = lax.axis_index("blk") * blocks_dev
     query_rows, key_rows, value_rows = (
-        lax.all_to_all(queries, "uly", split_axis=1, concat_axis=0, tiled=True),
+        recast_the_chains(queries),
         lax.all_to_all(keys, "uly", split_axis=1, concat_axis=0, tiled=True),
         lax.all_to_all(values, "uly", split_axis=1, concat_axis=0, tiled=True),
     )

time: 150 us -> 150 us (level)
  waiting for transfers between devices: 11.2 us -> 0.13 us
  starting transfers between devices: 3.63 us -> 11.3 us
  local copies, waits for them, and re-layouts: 24.3 us -> 28.4 us
    ppermute x0 -> x7, starting transfers between devices: none -> 11.3 us  [start_the_groups(): block_now = lax.ppermute(block_now, axis_name=along_axis, perm=tray)]
    all_to_all x1 -> x0, waiting for transfers between devices: 8.31 us -> none  [local(): lax.all_to_all(queries, 'uly', split_axis=1, concat_axis=0, tiled=True)]
    all_to_all x1 -> x0, starting transfers between devices: 3.59 us -> none  [local(): lax.all_to_all(queries, 'uly', split_axis=1, concat_axis=0, tiled=True)]
    dynamic_update_slice x0 -> x8, local copies, waits for them, and re-layouts: none -> 3.55 us  [start_the_groups(): lax.dynamic_update_slice_in_dim(a_now, block_now, (block_out ^ c) * spare...]
    all_gather x1, waiting for transfers between devices: 2.84 us -> 0.02 us  [local(): values_all = lax.all_gather(value_rows, 'blk', axis=0, tiled=True)]
  transfers between devices with their start and end apart: 3 -> 9, of which waited for: 2 -> 1; matrix products, arithmetic and copies ran while one was open for 5% -> 8% of each run, Pallas kernels for 0% -> 0%
where the time goes in v1:
time: 150 us; the launch traced here: 149 us
  blocking collectives  41.9 us (28%)
  matrix products  39.5 us (26%)
  local copies, waits for them, and re-layouts  28.4 us (19%)
  between operations  13.7 us (9%)
  other arithmetic  13.5 us (9%)
  starting transfers between devices  11.3 us (8%)
    dot_general x8, matrix products, attend_block(): jnp.einsum('abd,asjd->absj', query_group, key_slots, preferred_element_ty...  23 us
    dot_general x8, matrix products, attend_block(): jnp.einsum('absj,asjd->abd', rounded, value_slots, preferred_element_type...  16.4 us
    all_to_all x1, blocking collectives, local(): lax.all_to_all(keys, 'uly', split_axis=1, concat_axis=0, tiled=True)  16.1 us
    all_to_all x1, blocking collectives, local(): lax.all_to_all(result, 'uly', split_axis=0, concat_axis=1, tiled=True)  13.8 us
    reshape x5, local copies, waits for them, and re-layouts, head_major(): token_rows.reshape(token_rows.shape[0] // BLOCK, BLOCK, heads_local, head...  12.3 us
    all_to_all x1, blocking collectives, local(): lax.all_to_all(values, 'uly', split_axis=1, concat_axis=0, tiled=True)  12.1 us
    ppermute x7, starting transfers between devices, start_the_groups(): block_now = lax.ppermute(block_now, axis_name=along_axis, perm=tray)  11.3 us
    gather x3, local copies, waits for them, and re-layouts, select_blocks(): return jnp.take(source, chosen, axis=0)  6.75 us
  transfers between devices with their start and end apart: 9, of which 1 were waited for; matrix products, arithmetic and copies ran while one was open for 8% of the time, Pallas kernels for 0%

profile of v1, /device:TPU:0, one launch (start us, length us, event | category | flops | bytes accessed | tf_op | source)
XLA Modules:
  0.0 148.9 jit_solution(1581803181235399956)
XLA Ops:
  6.5 1.0 copy.84
  7.6 16.1 %all_to_all.57 = bf16[64,8,256]{2,0,1:T(8,128)(2,1)} all-to-all(bf16[64,8,256]{2,0,1:T(8,128)(2,1)S(1)} %bitcast.97), channel_id=1, replica_groups=mesh['uly'=8,'blk'=4] {'uly'}, dimensions={1} | all-to-all | bytes 524288 | tf_op jit(solution)/shard_map/all_to_all | solution.py:73
  23.8 1.0 copy.83
  24.7 12.1 %all_to_all.58 = bf16[64,8,256]{2,0,1:T(8,128)(2,1)} all-to-all(bf16[64,8,256]{2,0,1:T(8,128)(2,1)S(1)} %bitcast.98), channel_id=1, replica_groups=mesh['uly'=8,'blk'=4] {'uly'}, dimensions={1} | all-to-all | bytes 524288 | tf_op jit(solution)/shard_map/all_to_all | solution.py:74
  36.9 1.5 %collective-permute-start = (bf16[64,256]{1,0:T(8,128)(2,1)S(1)}, bf16[64,256]{1,0:T(8,128)(2,1)S(1)}, u32[]{:S(2)}, u32[]{:S(2)}) collective-permute-start(bf16[64,256]{1,0:T(8,128)(2,1)S(1)} %get-tuple-element.93), channel_id=1, source_target_pairs={{0,4},{4,0},{8,12},{12,8},{16,20},{20,16},{24,28},{28,24},{1,5},{5... | collective-permute-start | bytes 98312 | tf_op jit(solution)/shard_map/ppermute | solution.py:25
  38.5 2.0 %collective-permute-start.2 = (bf16[64,256]{1,0:T(8,128)(2,1)S(1)}, bf16[64,256]{1,0:T(8,128)(2,1)S(1)}, u32[]{:S(2)}, u32[]{:S(2)}) collective-permute-start(bf16[64,256]{1,0:T(8,128)(2,1)S(1)} %get-tuple-element.91), channel_id=1, source_target_pairs={{0,12},{4,8},{8,4},{12,0},{16,28},{20,24},{24,20},{28,16},{1,13},{... | collective-permute-start | bytes 98312 | tf_op jit(solution)/shard_map/ppermute | solution.py:25
  40.5 1.1 collective-permute-start.3
  41.5 2.8 %collective-permute-start.4 = (bf16[64,256]{1,0:T(8,128)(2,1)S(1)}, bf16[64,256]{1,0:T(8,128)(2,1)S(1)}, u32[]{:S(2)}, u32[]{:S(2)}) collective-permute-start(bf16[64,256]{1,0:T(8,128)(2,1)S(1)} %get-tuple-element.89), channel_id=1, source_target_pairs={{0,20},{4,16},{8,28},{12,24},{16,4},{20,0},{24,12},{28,8},{1,21},{... | collective-permute-start | bytes 98312 | tf_op jit(solution)/shard_map/ppermute | solution.py:25
  44.4 1.5 collective-permute-start.5
  45.8 2.4 %collective-permute-start.6 = (bf16[64,256]{1,0:T(8,128)(2,1)S(1)}, bf16[64,256]{1,0:T(8,128)(2,1)S(1)}, u32[]{:S(2)}, u32[]{:S(2)}) collective-permute-start(bf16[64,256]{1,0:T(8,128)(2,1)S(1)} %get-tuple-element.88), channel_id=1, source_target_pairs={{0,28},{4,24},{8,20},{12,16},{16,12},{20,8},{24,4},{28,0},{1,29},{... | collective-permute-start | bytes 98312 | tf_op jit(solution)/shard_map/ppermute | solution.py:25
  48.3 0.1 copy.44
  48.6 0.3 dynamic_update_slice.28
  48.9 0.1 copy.45
  49.0 0.6 dynamic_update_slice.29
  49.6 0.1 copy.46
  49.7 0.3 dynamic_update_slice.30
  50.1 0.1 copy.47
  50.2 0.6 dynamic_update_slice.31
  50.8 0.1 copy.48
  50.9 0.3 dynamic_update_slice.32
  51.3 0.1 copy.49
  51.4 0.6 dynamic_update_slice.33
  52.0 0.1 copy.50
  52.1 0.3 dynamic_update_slice.34
  52.4 0.1 copy.51
  52.6 0.5 dynamic_update_slice.35
  53.2 0.8 copy.52
  53.9 3.3 %reshape.146 = bf16[16,128,4,64]{3,2,1,0:T(4,128)(2,1)S(1)} reshape(bf16[2048,256]{1,0:T(8,128)(2,1)} %all-gather.3.cloned.1.call-done) | data formatting | bytes 2097152 | tf_op jit(solution)/shard_map/reshape | solution.py:34
  57.3 1.4 copy.55
  58.7 4.4 %reshape.147 = bf16[16,128,4,64]{3,2,1,0:T(4,128)(2,1)} reshape(bf16[2048,256]{1,0:T(8,128)(2,1)} %all-gather.5.cloned.1.call-done) | data formatting | bytes 2097152 | tf_op jit(solution)/shard_map/reshape | solution.py:34
  63.1 3.0 %copy.58 = bf16[16,128,4,64]{1,3,0,2:T(8,128)(2,1)S(1)} copy(bf16[16,128,4,64]{3,2,1,0:T(4,128)(2,1)} %reshape.147) | data formatting | bytes 2097152 | tf_op jit(solution)/shard_map/reshape | solution.py:34
  66.2 3.3 %gather_fusion = bf16[256,128,64]{1,2,0:T(8,128)(2,1)} fusion(bf16[4,16,128,64]{2,3,1,0:T(8,128)(2,1)S(1)} %bitcast.86, s32[256]{0:T(256)S(1)} %reshape.135), kind=kCustom, calls=%fused_computation.clone | custom fusion | bytes 8390656 | tf_op jit(solution)/shard_map/vmap(jit(_take))/gather | solution.py:40
  69.5 3.4 %gather_fusion.1 = bf16[256,128,64]{1,2,0:T(8,128)(2,1)} fusion(bf16[4,16,128,64]{2,3,1,0:T(8,128)(2,1)S(1)} %bitcast.87, s32[256]{0:T(256)S(1)} %reshape.135), kind=kCustom, calls=%fused_computation.1.clone | custom fusion | bytes 8390656 | tf_op jit(solution)/shard_map/vmap(jit(_take))/gather | solution.py:40
  72.9 5.9 %broadcast_select_fusion = (bf16[4,4,16,128,64]{3,4,2,1,0:T(8,128)(2,1)}, bf16[4,4,16,128,64]{3,4,2,1,0:T(8,128)(2,1)}) fusion(bf16[4,4,16,128,64]{3,4,2,1,0:T(8,128)(2,1)} %bitcast.89, pred[4,4,16]{2,1,0:T(4,128)(4,1)S(1)} %maximum_compare_fusion, bf16[4,4,16,128,64]{3,4,2,1,0:T(8,128)(2,1)} %bitcast.88), kind=kLoop, calls=%fused_computation.33 | loop fusion | flops 4194304 | bytes 16777472 | tf_op jit(solution)/shard_map/vmap(jit(_take))/select_n | solution.py:40
  78.8 47.9 %while.10 = (s32[]{:T(128)}, bf16[8,2,128,64]{2,1,0,3:T(2,128)(2,1)S(1)}, s32[8,2,16]{2,1,0:T(2,128)S(1)}, s32[8,2]{1,0:T(8,128)S(1)}, bf16[8,2,128,64]{2,3,1,0:...) while((s32[]{:T(128)}, ...), condition=%wide.region_3.5_spmd, body=%wide.region_0.4_spmd.sunk | while | flops 142118752 | bytes 7548157 | solution.py:93
  78.9 2.9 %fusion.31 = (f32[2,128]{1,0:T(2,128)S(1)}, f32[2,128,16,128]{1,3,2,0:T(8,128)S(1)}) fusion(bf16[8,2,16,128,64]{3,4,2,1,0:T(8,128)(2,1)} %get-tuple-element.166, s32[]{:T(128)} %get-tuple-element.153, bf16[8,2,128,64]{2,3,1,0:T(8,128)(2,1)} %get-tuple-element.165, s32[2,128]{1,0:T(2,128)S(1)} %iota_add_fusion.4, ...), kind=kOutput, calls=%fused_computation.48.clone.1 | convolution fusion | flops 69730048 | bytes 2673696 | tf_op jit(solution)/shard_map/while/body/eval_jaxpr/abd,asjd->absj/dot_general | solution.py:47
  81.8 0.8 fusion.32
  82.6 2.1 %fusion.33 = bf16[1,2,128,64]{2,3,1,0:T(8,128)(2,1)S(1)} fusion(f32[2,128,16,128]{1,3,2,0:T(8,128)S(1)} %get-tuple-element.143, f32[2,128]{1,0:T(2,128)S(1)} %get-tuple-element.144, s32[2,128]{1,0:T(2,128)S(1)} %iota_add_fusion.4, s32[2,16,128]{2,1,0:T(8,128)S(1)} %iota_add_fusion.5, pred[2,16]{1,0:T(4,128)(4,1)S(1)} %compare_bitcast_fusion.2, ...), kind=kOutput, calls=%fused_computation.10.clone.1 | convolution fusion | flops 69763072 | bytes 2674208 | tf_op jit(solution)/shard_map/while/body/eval_jaxpr/absj,asjd->abd/dot_general | solution.py:61
  84.9 2.9 %fusion.31 = (f32[2,128]{1,0:T(2,128)S(1)}, f32[2,128,16,128]{1,3,2,0:T(8,128)S(1)}) fusion(bf16[8,2,16,128,64]{3,4,2,1,0:T(8,128)(2,1)} %get-tuple-element.166, s32[]{:T(128)} %get-tuple-element.153, bf16[8,2,128,64]{2,3,1,0:T(8,128)(2,1)} %get-tuple-element.165, s32[2,128]{1,0:T(2,128)S(1)} %iota_add_fusion.4, ...), kind=kOutput, calls=%fused_computation.48.clone.1 | convolution fusion | flops 69730048 | bytes 2673696 | tf_op jit(solution)/shard_map/while/body/eval_jaxpr/abd,asjd->absj/dot_general | solution.py:47
  87.8 0.8 fusion.32
  88.6 2.1 %fusion.33 = bf16[1,2,128,64]{2,3,1,0:T(8,128)(2,1)S(1)} fusion(f32[2,128,16,128]{1,3,2,0:T(8,128)S(1)} %get-tuple-element.143, f32[2,128]{1,0:T(2,128)S(1)} %get-tuple-element.144, s32[2,128]{1,0:T(2,128)S(1)} %iota_add_fusion.4, s32[2,16,128]{2,1,0:T(8,128)S(1)} %iota_add_fusion.5, pred[2,16]{1,0:T(4,128)(4,1)S(1)} %compare_bitcast_fusion.2, ...), kind=kOutput, calls=%fused_computation.10.clone.1 | convolution fusion | flops 69763072 | bytes 2674208 | tf_op jit(solution)/shard_map/while/body/eval_jaxpr/absj,asjd->abd/dot_general | solution.py:61
  90.9 2.9 %fusion.31 = (f32[2,128]{1,0:T(2,128)S(1)}, f32[2,128,16,128]{1,3,2,0:T(8,128)S(1)}) fusion(bf16[8,2,16,128,64]{3,4,2,1,0:T(8,128)(2,1)} %get-tuple-element.166, s32[]{:T(128)} %get-tuple-element.153, bf16[8,2,128,64]{2,3,1,0:T(8,128)(2,1)} %get-tuple-element.165, s32[2,128]{1,0:T(2,128)S(1)} %iota_add_fusion.4, ...), kind=kOutput, calls=%fused_computation.48.clone.1 | convolution fusion | flops 69730048 | bytes 2673696 | tf_op jit(solution)/shard_map/while/body/eval_jaxpr/abd,asjd->absj/dot_general | solution.py:47
  93.8 0.8 fusion.32
  94.6 2.1 %fusion.33 = bf16[1,2,128,64]{2,3,1,0:T(8,128)(2,1)S(1)} fusion(f32[2,128,16,128]{1,3,2,0:T(8,128)S(1)} %get-tuple-element.143, f32[2,128]{1,0:T(2,128)S(1)} %get-tuple-element.144, s32[2,128]{1,0:T(2,128)S(1)} %iota_add_fusion.4, s32[2,16,128]{2,1,0:T(8,128)S(1)} %iota_add_fusion.5, pred[2,16]{1,0:T(4,128)(4,1)S(1)} %compare_bitcast_fusion.2, ...), kind=kOutput, calls=%fused_computation.10.clone.1 | convolution fusion | flops 69763072 | bytes 2674208 | tf_op jit(solution)/shard_map/while/body/eval_jaxpr/absj,asjd->abd/dot_general | solution.py:61
  96.9 2.9 %fusion.31 = (f32[2,128]{1,0:T(2,128)S(1)}, f32[2,128,16,128]{1,3,2,0:T(8,128)S(1)}) fusion(bf16[8,2,16,128,64]{3,4,2,1,0:T(8,128)(2,1)} %get-tuple-element.166, s32[]{:T(128)} %get-tuple-element.153, bf16[8,2,128,64]{2,3,1,0:T(8,128)(2,1)} %get-tuple-element.165, s32[2,128]{1,0:T(2,128)S(1)} %iota_add_fusion.4, ...), kind=kOutput, calls=%fused_computation.48.clone.1 | convolution fusion | flops 69730048 | bytes 2673696 | tf_op jit(solution)/shard_map/while/body/eval_jaxpr/abd,asjd->absj/dot_general | solution.py:47
  99.8 0.8 fusion.32
  100.6 2.1 %fusion.33 = bf16[1,2,128,64]{2,3,1,0:T(8,128)(2,1)S(1)} fusion(f32[2,128,16,128]{1,3,2,0:T(8,128)S(1)} %get-tuple-element.143, f32[2,128]{1,0:T(2,128)S(1)} %get-tuple-element.144, s32[2,128]{1,0:T(2,128)S(1)} %iota_add_fusion.4, s32[2,16,128]{2,1,0:T(8,128)S(1)} %iota_add_fusion.5, pred[2,16]{1,0:T(4,128)(4,1)S(1)} %compare_bitcast_fusion.2, ...), kind=kOutput, calls=%fused_computation.10.clone.1 | convolution fusion | flops 69763072 | bytes 2674208 | tf_op jit(solution)/shard_map/while/body/eval_jaxpr/absj,asjd->abd/dot_general | solution.py:61
  102.9 2.9 %fusion.31 = (f32[2,128]{1,0:T(2,128)S(1)}, f32[2,128,16,128]{1,3,2,0:T(8,128)S(1)}) fusion(bf16[8,2,16,128,64]{3,4,2,1,0:T(8,128)(2,1)} %get-tuple-element.166, s32[]{:T(128)} %get-tuple-element.153, bf16[8,2,128,64]{2,3,1,0:T(8,128)(2,1)} %get-tuple-element.165, s32[2,128]{1,0:T(2,128)S(1)} %iota_add_fusion.4, ...), kind=kOutput, calls=%fused_computation.48.clone.1 | convolution fusion | flops 69730048 | bytes 2673696 | tf_op jit(solution)/shard_map/while/body/eval_jaxpr/abd,asjd->absj/dot_general | solution.py:47
  105.8 0.8 fusion.32
  106.6 2.1 %fusion.33 = bf16[1,2,128,64]{2,3,1,0:T(8,128)(2,1)S(1)} fusion(f32[2,128,16,128]{1,3,2,0:T(8,128)S(1)} %get-tuple-element.143, f32[2,128]{1,0:T(2,128)S(1)} %get-tuple-element.144, s32[2,128]{1,0:T(2,128)S(1)} %iota_add_fusion.4, s32[2,16,128]{2,1,0:T(8,128)S(1)} %iota_add_fusion.5, pred[2,16]{1,0:T(4,128)(4,1)S(1)} %compare_bitcast_fusion.2, ...), kind=kOutput, calls=%fused_computation.10.clone.1 | convolution fusion | flops 69763072 | bytes 2674208 | tf_op jit(solution)/shard_map/while/body/eval_jaxpr/absj,asjd->abd/dot_general | solution.py:61
  108.9 2.9 %fusion.31 = (f32[2,128]{1,0:T(2,128)S(1)}, f32[2,128,16,128]{1,3,2,0:T(8,128)S(1)}) fusion(bf16[8,2,16,128,64]{3,4,2,1,0:T(8,128)(2,1)} %get-tuple-element.166, s32[]{:T(128)} %get-tuple-element.153, bf16[8,2,128,64]{2,3,1,0:T(8,128)(2,1)} %get-tuple-element.165, s32[2,128]{1,0:T(2,128)S(1)} %iota_add_fusion.4, ...), kind=kOutput, calls=%fused_computation.48.clone.1 | convolution fusion | flops 69730048 | bytes 2673696 | tf_op jit(solution)/shard_map/while/body/eval_jaxpr/abd,asjd->absj/dot_general | solution.py:47
  111.8 0.8 fusion.32
  112.6 2.1 %fusion.33 = bf16[1,2,128,64]{2,3,1,0:T(8,128)(2,1)S(1)} fusion(f32[2,128,16,128]{1,3,2,0:T(8,128)S(1)} %get-tuple-element.143, f32[2,128]{1,0:T(2,128)S(1)} %get-tuple-element.144, s32[2,128]{1,0:T(2,128)S(1)} %iota_add_fusion.4, s32[2,16,128]{2,1,0:T(8,128)S(1)} %iota_add_fusion.5, pred[2,16]{1,0:T(4,128)(4,1)S(1)} %compare_bitcast_fusion.2, ...), kind=kOutput, calls=%fused_computation.10.clone.1 | convolution fusion | flops 69763072 | bytes 2674208 | tf_op jit(solution)/shard_map/while/body/eval_jaxpr/absj,asjd->abd/dot_general | solution.py:61
  114.9 2.9 %fusion.31 = (f32[2,128]{1,0:T(2,128)S(1)}, f32[2,128,16,128]{1,3,2,0:T(8,128)S(1)}) fusion(bf16[8,2,16,128,64]{3,4,2,1,0:T(8,128)(2,1)} %get-tuple-element.166, s32[]{:T(128)} %get-tuple-element.153, bf16[8,2,128,64]{2,3,1,0:T(8,128)(2,1)} %get-tuple-element.165, s32[2,128]{1,0:T(2,128)S(1)} %iota_add_fusion.4, ...), kind=kOutput, calls=%fused_computation.48.clone.1 | convolution fusion | flops 69730048 | bytes 2673696 | tf_op jit(solution)/shard_map/while/body/eval_jaxpr/abd,asjd->absj/dot_general | solution.py:47
  117.8 0.8 fusion.32
  118.6 2.1 %fusion.33 = bf16[1,2,128,64]{2,3,1,0:T(8,128)(2,1)S(1)} fusion(f32[2,128,16,128]{1,3,2,0:T(8,128)S(1)} %get-tuple-element.143, f32[2,128]{1,0:T(2,128)S(1)} %get-tuple-element.144, s32[2,128]{1,0:T(2,128)S(1)} %iota_add_fusion.4, s32[2,16,128]{2,1,0:T(8,128)S(1)} %iota_add_fusion.5, pred[2,16]{1,0:T(4,128)(4,1)S(1)} %compare_bitcast_fusion.2, ...), kind=kOutput, calls=%fused_computation.10.clone.1 | convolution fusion | flops 69763072 | bytes 2674208 | tf_op jit(solution)/shard_map/while/body/eval_jaxpr/absj,asjd->abd/dot_general | solution.py:61
  120.9 2.9 %fusion.31 = (f32[2,128]{1,0:T(2,128)S(1)}, f32[2,128,16,128]{1,3,2,0:T(8,128)S(1)}) fusion(bf16[8,2,16,128,64]{3,4,2,1,0:T(8,128)(2,1)} %get-tuple-element.166, s32[]{:T(128)} %get-tuple-element.153, bf16[8,2,128,64]{2,3,1,0:T(8,128)(2,1)} %get-tuple-element.165, s32[2,128]{1,0:T(2,128)S(1)} %iota_add_fusion.4, ...), kind=kOutput, calls=%fused_computation.48.clone.1 | convolution fusion | flops 69730048 | bytes 2673696 | tf_op jit(solution)/shard_map/while/body/eval_jaxpr/abd,asjd->absj/dot_general | solution.py:47
  123.8 0.8 fusion.32
  124.6 2.1 %fusion.33 = bf16[1,2,128,64]{2,3,1,0:T(8,128)(2,1)S(1)} fusion(f32[2,128,16,128]{1,3,2,0:T(8,128)S(1)} %get-tuple-element.143, f32[2,128]{1,0:T(2,128)S(1)} %get-tuple-element.144, s32[2,128]{1,0:T(2,128)S(1)} %iota_add_fusion.4, s32[2,16,128]{2,1,0:T(8,128)S(1)} %iota_add_fusion.5, pred[2,16]{1,0:T(4,128)(4,1)S(1)} %compare_bitcast_fusion.2, ...), kind=kOutput, calls=%fused_computation.10.clone.1 | convolution fusion | flops 69763072 | bytes 2674208 | tf_op jit(solution)/shard_map/while/body/eval_jaxpr/absj,asjd->abd/dot_general | solution.py:61
  126.7 0.1 reshape.111
  126.8 0.4 copy.72
  127.2 0.3 reshape.148
  127.5 13.8 %all_to_all.59 = bf16[8,64,256]{2,1,0:T(8,128)(2,1)S(1)} all-to-all(bf16[8,64,256]{2,1,0:T(8,128)(2,1)S(1)} %reshape.148), channel_id=1, replica_groups=mesh['uly'=8,'blk'=4] {'uly'}, dimensions={0} | all-to-all | bytes 524288 | tf_op jit(solution)/shard_map/all_to_all | solution.py:98
  141.3 0.7 copy.79
  (76 shorter events, 2.3 us)
Async XLA Ops:
  6.5 30.3 %copy-start = (bf16[64,2048]{1,0:T(8,128)(2,1)S(1)}, bf16[64,2048]{1,0:T(8,128)(2,1)}, u32[]{:S(2)}) copy-start(bf16[64,2048]{1,0:T(8,128)(2,1)} %param.8) | copy-start | bytes 786436
  6.5 37.8 %copy-start.1 = (s32[4,4,16]{2,1,0:T(4,128)S(1)}, s32[4,4,16]{2,1,0:T(4,128)}, u32[]{:S(2)}) copy-start(s32[4,4,16]{2,1,0:T(4,128)} %param.11) | copy-start | bytes 3076
  6.5 47.4 %all-gather.3.cloned.1.call-start = ((), (), s32[]{:S(2)}) async-start(), calls=%async_computation.3 | async-start | bytes 1310720 | tf_op jit(solution)/shard_map/all_gather | solution.py:76
  23.7 35.0 %all-gather.5.cloned.1.call-start = ((), (), s32[]{:S(2)}) async-start(), calls=%async_computation.4 | async-start | bytes 1310720 | tf_op jit(solution)/shard_map/all_gather | solution.py:77
  36.9 7.4 %collective-permute-start = (bf16[64,256]{1,0:T(8,128)(2,1)S(1)}, bf16[64,256]{1,0:T(8,128)(2,1)S(1)}, u32[]{:S(2)}, u32[]{:S(2)}) collective-permute-start(bf16[64,256]{1,0:T(8,128)(2,1)S(1)} %get-tuple-element.93), channel_id=1, source_target_pairs={{0,4},{4,0},{8,12},{12,8},{16,20},{20,16},{24,28},{28,24},{1,5},{5... | collective-permute-start | bytes 98312 | tf_op jit(solution)/shard_map/ppermute | solution.py:25
  38.5 7.4 %collective-permute-start.1 = (bf16[64,256]{1,0:T(8,128)(2,1)S(1)}, bf16[64,256]{1,0:T(8,128)(2,1)S(1)}, u32[]{:S(2)}, u32[]{:S(2)}) collective-permute-start(bf16[64,256]{1,0:T(8,128)(2,1)S(1)} %get-tuple-element.92), channel_id=1, source_target_pairs={{0,8},{4,12},{8,0},{12,4},{16,24},{20,28},{24,16},{28,20},{1,9},{5... | collective-permute-start | bytes 98312 | tf_op jit(solution)/shard_map/ppermute | solution.py:25
  38.5 11.6 %collective-permute-start.2 = (bf16[64,256]{1,0:T(8,128)(2,1)S(1)}, bf16[64,256]{1,0:T(8,128)(2,1)S(1)}, u32[]{:S(2)}, u32[]{:S(2)}) collective-permute-start(bf16[64,256]{1,0:T(8,128)(2,1)S(1)} %get-tuple-element.91), channel_id=1, source_target_pairs={{0,12},{4,8},{8,4},{12,0},{16,28},{20,24},{24,20},{28,16},{1,13},{... | collective-permute-start | bytes 98312 | tf_op jit(solution)/shard_map/ppermute | solution.py:25
  40.5 10.3 %collective-permute-start.3 = (bf16[64,256]{1,0:T(8,128)(2,1)S(1)}, bf16[64,256]{1,0:T(8,128)(2,1)S(1)}, u32[]{:S(2)}, u32[]{:S(2)}) collective-permute-start(bf16[64,256]{1,0:T(8,128)(2,1)S(1)} %get-tuple-element.90), channel_id=1, source_target_pairs={{0,16},{4,20},{8,24},{12,28},{16,0},{20,4},{24,8},{28,12},{1,17},{... | collective-permute-start | bytes 98312 | tf_op jit(solution)/shard_map/ppermute | solution.py:25
  41.5 9.7 %collective-permute-start.4 = (bf16[64,256]{1,0:T(8,128)(2,1)S(1)}, bf16[64,256]{1,0:T(8,128)(2,1)S(1)}, u32[]{:S(2)}, u32[]{:S(2)}) collective-permute-start(bf16[64,256]{1,0:T(8,128)(2,1)S(1)} %get-tuple-element.89), channel_id=1, source_target_pairs={{0,20},{4,16},{8,28},{12,24},{16,4},{20,0},{24,12},{28,8},{1,21},{... | collective-permute-start | bytes 98312 | tf_op jit(solution)/shard_map/ppermute | solution.py:25
  44.4 7.6 %collective-permute-start.5 = (bf16[64,256]{1,0:T(8,128)(2,1)S(1)}, bf16[64,256]{1,0:T(8,128)(2,1)S(1)}, u32[]{:S(2)}, u32[]{:S(2)}) collective-permute-start(bf16[64,256]{1,0:T(8,128)(2,1)S(1)} %get-tuple-element.95), channel_id=1, source_target_pairs={{0,24},{4,28},{8,16},{12,20},{16,8},{20,12},{24,0},{28,4},{1,25},{... | collective-permute-start | bytes 98312 | tf_op jit(solution)/shard_map/ppermute | solution.py:25
  45.8 6.6 %collective-permute-start.6 = (bf16[64,256]{1,0:T(8,128)(2,1)S(1)}, bf16[64,256]{1,0:T(8,128)(2,1)S(1)}, u32[]{:S(2)}, u32[]{:S(2)}) collective-permute-start(bf16[64,256]{1,0:T(8,128)(2,1)S(1)} %get-tuple-element.88), channel_id=1, source_target_pairs={{0,28},{4,24},{8,20},{12,16},{16,12},{20,8},{24,4},{28,0},{1,29},{... | collective-permute-start | bytes 98312 | tf_op jit(solution)/shard_map/ppermute | solution.py:25
Sparse Core Ops, SparseCore 0:
  23.8 15.6 all-gather.2
  41.1 16.6 all-gather.4
